TPU v7x, 256 devices: a whole 4x4x8 slice. The times are simulated.
256 devices in a mesh: row: 32 (over y, x, core), col: 8 (over z).
Axes of the slice: x: 4, y: 4, z: 8, core: 2. Of those that a mesh axis runs over, the one named last changes fastest.
Arguments:
- inputs: bfloat16 [4096, 5120], P('row', 'col'), may hold values from -6 to 6
- grad_out: bfloat16 [4096, 5120], P('row', 'col'), may hold values from -6 to 6
- pre_act: bfloat16 [4096, 13824], P('col', 'row'), may hold values from -6 to 6
- w_in: bfloat16 [13824, 5120], P('row', 'col'), may hold values from -0.078125 to 0.078125
- w_out: bfloat16 [13824, 5120], P('row', 'col'), may hold values from -0.0546875 to 0.0546875
- row_in_prev: float32 [13824], P('row'), may hold values from 204.8 to 24576, as said below
- col_in_prev: float32 [5120], P('col'), may hold values from 204.8 to 24576, as said below
- row_out_prev: float32 [13824], P('row'), may hold values from 204.8 to 24576, as said below
- col_out_prev: float32 [5120], P('col'), may hold values from 204.8 to 24576, as said below
Outputs:
- input_grad: bfloat16 [4096, 5120], P('row', 'col')
- update_in: float32 [13824, 5120], P('row', 'col')
- row_in: float32 [13824], P('row')
- col_in: float32 [5120], P('col')
- update_out: float32 [13824, 5120], P('row', 'col')
- row_out: float32 [13824], P('row')
- col_out: float32 [5120], P('col')
Inputs may be any that keep to these rules, and one draw needn't show every extreme that they name: `row_in_prev`: positive. `col_in_prev`: positive. `row_out_prev`: positive. `col_out_prev`: positive.
All inputs are finite; a program needn't handle non-finite values.
Results may differ from a plain program's by a relative error of at most 0.023.
Values may be sent and summed in bfloat16 or wider, within the bound.
A program may use at most 128 MiB of HBM per device.

v0:
```python
import math
import jax
import jax.numpy as jnp
from jax import lax
from jax.sharding import PartitionSpec as P

D = 5120
FF = 13824
decay_rate = 0.8
epsilon_sq = 1e-30
clip_limit = 0.25
gelu_coef = 0.044715
root_coef = math.sqrt(2.0 / math.pi)


def gelu_parts(pre_float):
    tanh_value = jnp.tanh(root_coef * (pre_float + gelu_coef * pre_float * pre_float * pre_float))
    value = 0.5 * pre_float * (1.0 + tanh_value)
    slope = 0.5 * (1.0 + tanh_value) + 0.5 * pre_float * (
        1.0 - tanh_value * tanh_value
    ) * root_coef * (1.0 + 3.0 * gelu_coef * pre_float * pre_float)
    return (value, slope)


def contract_last(left, right):
    return lax.dot_general(
        left, right, (((1,), (1,)), ((), ())), preferred_element_type=jnp.float32
    )


def contract_first(left, right):
    return lax.dot_general(
        left, right, (((0,), (0,)), ((), ())), preferred_element_type=jnp.float32
    )


def row_moment(row_sum, row_prev):
    return decay_rate * row_prev + (1.0 - decay_rate) * (row_sum / D + epsilon_sq)


def col_moment(col_sum, col_prev):
    return decay_rate * col_prev + (1.0 - decay_rate) * (col_sum / FF + epsilon_sq)


def per_device(
    inputs, grad_out, pre_act, w_in, w_out, row_in_prev, col_in_prev, row_out_prev, col_out_prev
):
    grad_all, input_all = (
        lax.all_gather(grad_out, "row", axis=0, tiled=True),
        lax.all_gather(inputs, "row", axis=0, tiled=True),
    )
    token_count = float(inputs.shape[0] * lax.axis_size("row"))
    rows_here = grad_all
    hidden_grad = lax.psum_scatter(
        contract_last(rows_here, w_out).astype(jnp.bfloat16), "col", scatter_dimension=0, tiled=True
    ).astype(jnp.float32)
    value, slope = gelu_parts(pre_act.astype(jnp.float32))
    act = value.astype(jnp.bfloat16)
    pre_grad = (hidden_grad * slope).astype(jnp.bfloat16)
    act_all, pre_grad_all = (
        lax.all_gather(act, "col", axis=0, tiled=True),
        lax.all_gather(pre_grad, "col", axis=0, tiled=True),
    )
    grad_w_out = contract_first(act_all, grad_all)
    grad_w_in = contract_first(pre_grad_all, input_all)
    rows_here = pre_grad_all
    input_sum = lax.psum_scatter(
        jnp.dot(rows_here, w_in, preferred_element_type=jnp.float32).astype(jnp.bfloat16),
        "row",
        scatter_dimension=0,
        tiled=True,
    )
    square_in = grad_w_in * grad_w_in
    square_out = grad_w_out * grad_w_out
    row_sums = lax.psum((jnp.sum(square_in, axis=1), jnp.sum(square_out, axis=1)), "col")
    row_in = row_moment(row_sums[0], row_in_prev)
    row_out = row_moment(row_sums[1], row_out_prev)
    col_sums = lax.psum((jnp.sum(square_in, axis=0), jnp.sum(square_out, axis=0)), "row")
    col_in = col_moment(col_sums[0], col_in_prev)
    col_out = col_moment(col_sums[1], col_out_prev)
    raw_in = grad_w_in / jnp.sqrt(row_in[:, None] * col_in[None, :] / token_count)
    raw_out = grad_w_out / jnp.sqrt(row_out[:, None] * col_out[None, :] / token_count)
    norms = lax.psum((jnp.sum(raw_in * raw_in), jnp.sum(raw_out * raw_out)), ("row", "col"))
    total_in = norms[0]
    total_out = norms[1]
    rms_in = jnp.sqrt(total_in / (FF * D))
    rms_out = jnp.sqrt(total_out / (FF * D))
    update_in = raw_in / jnp.maximum(1.0, rms_in / clip_limit)
    update_out = raw_out / jnp.maximum(1.0, rms_out / clip_limit)
    return (input_sum, update_in, row_in, col_in, update_out, row_out, col_out)


def solution(mesh):
    return jax.shard_map(
        per_device,
        mesh=mesh,
        in_specs=(
            P("row", "col"),
            P("row", "col"),
            P("col", "row"),
            P("row", "col"),
            P("row", "col"),
            P("row"),
            P("col"),
            P("row"),
            P("col"),
        ),
        out_specs=(
            P("row", "col"),
            P("row", "col"),
            P("row"),
            P("col"),
            P("row", "col"),
            P("row"),
            P("col"),
        ),
        check_vma=False,
    )
```

profile of v0, /device:TPU:1, one launch (start us, length us, event | category | flops | bytes accessed | tf_op | source)
XLA Modules:
  0.0 452.0 jit_solution(9500882296809639069)
XLA Ops:
  7.2 0.0 copy-start
  7.2 0.0 all-gather.5.cloned.1.call-start
  7.2 0.7 all-gather.5.cloned.1.call-update
  7.9 0.0 reduce-scatter.3.cloned.1.call-start
  8.0 59.3 %all-gather.5.cloned.1.call-done = bf16[4096,640]{1,0:T(8,128)(2,1)} async-done(((bf16[128,640]{1,0:T(8,128)(2,1)}), bf16[4096,640]{1,0:T(8,128)(2,1)}) %all-gather.5.cloned.1.call-update) | async-done | bytes 5242896 | tf_op jit(solution)/shard_map/all_gather | solution.py:49
  67.3 7.4 %convolution_convert_fusion.1 = bf16[4096,432]{0,1:T(8,128)(2,1)} fusion(bf16[4096,640]{1,0:T(8,128)(2,1)} %all-gather.5.cloned.1.call-done, bf16[432,640]{1,0:T(8,128)(2,1)} %param.13), kind=kOutput, calls=%fused_computation.1 | convolution fusion | flops 2266693632 | bytes 9334784 | tf_op jit(solution)/shard_map/dot_general | solution.py:26
  74.7 0.0 reduce-scatter.3.cloned.1.call-update
  74.7 0.0 all-gather.7.cloned.1.call-start
  74.7 48.2 %reduce-scatter.3.cloned.1.call-done = bf16[512,432]{0,1:T(8,128)(2,1)} async-done(((bf16[4096,432]{0,1:T(8,128)(2,1)}), bf16[512,432]{0,1:T(8,128)(2,1)}) %reduce-scatter.3.cloned.1.call-update) | async-done | bytes 442384 | tf_op jit(solution)/shard_map/reduce_scatter | solution.py:54
  123.0 2.6 fusion.7
  125.6 0.0 all-gather.7.cloned.1.call-update
  125.6 0.0 all-gather.11.cloned.1.call-start
  125.6 0.5 all-gather.11.cloned.1.call-update
  126.2 0.0 all-gather.9.cloned.1.call-start
  126.2 0.5 all-gather.9.cloned.1.call-update
  126.8 0.0 reduce-scatter.5.cloned.1.call-start
  126.8 46.8 %all-gather.7.cloned.1.call-done = bf16[4096,432]{0,1:T(8,128)(2,1)} async-done(((bf16[512,432]{0,1:T(8,128)(2,1)}), bf16[4096,432]{0,1:T(8,128)(2,1)}) %all-gather.7.cloned.1.call-update) | async-done | bytes 3538960 | tf_op jit(solution)/shard_map/all_gather | solution.py:62
  173.6 7.9 %convolution_convert_fusion = bf16[4096,640]{1,0:T(8,128)(2,1)} fusion(bf16[4096,432]{0,1:T(8,128)(2,1)} %all-gather.7.cloned.1.call-done, bf16[432,640]{1,0:T(8,128)(2,1)S(1)} %copy-done), kind=kOutput, calls=%fused_computation | convolution fusion | flops 2267545600 | bytes 9334784 | tf_op jit(solution)/shard_map/dot_general | solution.py:68
  181.5 0.0 reduce-scatter.5.cloned.1.call-update
  181.5 41.8 %all-gather.11.cloned.1.call-done = bf16[4096,432]{0,1:T(8,128)(2,1)} async-done(((bf16[512,432]{0,1:T(8,128)(2,1)}), bf16[4096,432]{0,1:T(8,128)(2,1)}) %all-gather.11.cloned.1.call-update) | async-done | bytes 3538960 | tf_op jit(solution)/shard_map/all_gather | solution.py:61
  223.3 6.6 %multiply_reduce_fusion.3 = (f32[432]{0:T(512)S(1)}, f32[640]{0:T(1024)S(1)}, f32[432,640]{1,0:T(8,128)S(1)}) fusion(bf16[4096,432]{0,1:T(8,128)(2,1)} %all-gather.11.cloned.1.call-done, bf16[4096,640]{1,0:T(8,128)(2,1)} %all-gather.5.cloned.1.call-done), kind=kOutput, calls=%fused_computation.16 | convolution fusion | flops 2265752576 | bytes 9892032 | tf_op jit(solution)/shard_map/dot_general | solution.py:32
  229.9 47.6 %all-gather.9.cloned.1.call-done = bf16[4096,640]{1,0:T(8,128)(2,1)} async-done(((bf16[128,640]{1,0:T(8,128)(2,1)}), bf16[4096,640]{1,0:T(8,128)(2,1)}) %all-gather.9.cloned.1.call-update) | async-done | bytes 5242896 | tf_op jit(solution)/shard_map/all_gather | solution.py:50
  277.6 6.6 %multiply_reduce_fusion.5 = (f32[432]{0:T(512)S(1)}, f32[640]{0:T(1024)S(1)}, f32[432,640]{1,0:T(8,128)S(1)}) fusion(bf16[4096,432]{0,1:T(8,128)(2,1)} %all-gather.7.cloned.1.call-done, bf16[4096,640]{1,0:T(8,128)(2,1)} %all-gather.9.cloned.1.call-done), kind=kOutput, calls=%fused_computation.18 | convolution fusion | flops 2265752576 | bytes 9892032 | tf_op jit(solution)/shard_map/dot_general | solution.py:32
  284.1 63.8 %all-reduce.1 = (f32[640]{0:T(1024)S(1)}, f32[640]{0:T(1024)S(1)}) all-reduce(f32[640]{0:T(1024)S(1)} %get-tuple-element.10, f32[640]{0:T(1024)S(1)} %get-tuple-element.8), channel_id=1, replica_groups=mesh['row'=32,'col'=8] {'row'}, use_global_device_ids=true, to_apply=%region_5.0 | all-reduce | flops 1280 | bytes 10240 | tf_op jit(solution)/shard_map/psum | solution.py:78
  347.9 13.8 %all-reduce.2 = (f32[432]{0:T(512)S(1)}, f32[432]{0:T(512)S(1)}) all-reduce(f32[432]{0:T(512)S(1)} %get-tuple-element.9, f32[432]{0:T(512)S(1)} %get-tuple-element.7), channel_id=1, replica_groups=mesh['row'=32,'col'=8] {'col'}, use_global_device_ids=true, to_apply=%region_3.0 | all-reduce | flops 864 | bytes 6912 | tf_op jit(solution)/shard_map/psum | solution.py:75
  361.8 0.0 copy-start.5
  361.8 0.0 copy-start.2
  361.8 1.1 multiply_reduce_fusion
  362.9 1.1 multiply_reduce_fusion.1
  364.0 77.3 %all-reduce = (f32[]{:T(128)}, f32[]{:T(128)}) all-reduce(f32[]{:T(128)} %multiply_reduce_fusion.1, f32[]{:T(128)} %multiply_reduce_fusion), channel_id=1, replica_groups=mesh['row'=32,'col'=8] {'row','col'}, use_global_device_ids=true, to_apply=%region_7.0 | all-reduce | flops 2 | bytes 16 | tf_op jit(solution)/shard_map/psum | solution.py:83
  442.7 1.2 fusion.12
  444.0 1.2 fusion.11
  (20 shorter events, 0.1 us)
Async XLA Ops:
  7.2 166.5 %copy-start = (bf16[432,640]{1,0:T(8,128)(2,1)S(1)}, bf16[432,640]{1,0:T(8,128)(2,1)}, u32[]{:S(2)}) copy-start(bf16[432,640]{1,0:T(8,128)(2,1)} %param.12) | copy-start | bytes 1658884
  7.2 60.1 %all-gather.5.cloned.1.call-start = ((), (), s32[]{:S(2)}) async-start(), calls=%async_computation.2 | async-start | bytes 5406720 | tf_op jit(solution)/shard_map/all_gather | solution.py:49
  7.9 115.1 %reduce-scatter.3.cloned.1.call-start = ((), (), s32[]{:S(2)}) async-start(), calls=%async_computation.3 | async-start | bytes 3981312 | tf_op jit(solution)/shard_map/reduce_scatter | solution.py:54
  74.7 48.3 %copy-start.1 = (bf16[512,432]{0,1:T(8,128)(2,1)S(1)}, bf16[512,432]{0,1:T(8,128)(2,1)}, u32[]{:S(2)}) copy-start(bf16[512,432]{0,1:T(8,128)(2,1)} %param.11) | copy-start | bytes 1327108
  74.7 98.9 %all-gather.7.cloned.1.call-start = ((), (), s32[]{:S(2)}) async-start(), calls=%async_computation.4 | async-start | bytes 3981312 | tf_op jit(solution)/shard_map/all_gather | solution.py:62
  125.6 97.7 %all-gather.11.cloned.1.call-start = ((), (), s32[]{:S(2)}) async-start(), calls=%async_computation.7 | async-start | bytes 3981312 | tf_op jit(solution)/shard_map/all_gather | solution.py:61
  126.2 151.4 %all-gather.9.cloned.1.call-start = ((), (), s32[]{:S(2)}) async-start(), calls=%async_computation.6 | async-start | bytes 5406720 | tf_op jit(solution)/shard_map/all_gather | solution.py:50
  126.8 318.4 %reduce-scatter.5.cloned.1.call-start = ((), (), s32[]{:S(2)}) async-start(), calls=%async_computation.5 | async-start | bytes 5406720 | tf_op jit(solution)/shard_map/reduce_scatter | solution.py:67
  229.9 131.9 %copy-start.8 = (f32[432]{0:T(512)S(1)}, f32[432]{0:T(512)}, u32[]{:S(2)}) copy-start(f32[432]{0:T(512)} %param.16) | copy-start | bytes 5188
  229.9 131.9 %copy-start.9 = (f32[432]{0:T(512)S(1)}, f32[432]{0:T(512)}, u32[]{:S(2)}) copy-start(f32[432]{0:T(512)} %param.14) | copy-start | bytes 5188
  229.9 131.9 %copy-start.6 = (f32[640]{0:T(1024)S(1)}, f32[640]{0:T(1024)}, u32[]{:S(2)}) copy-start(f32[640]{0:T(1024)} %param.17) | copy-start | bytes 7684
  229.9 131.9 %copy-start.7 = (f32[640]{0:T(1024)S(1)}, f32[640]{0:T(1024)}, u32[]{:S(2)}) copy-start(f32[640]{0:T(1024)} %param.15) | copy-start | bytes 7684
  361.8 80.9 %copy-start.4 = (f32[432]{0:T(512)}, f32[432]{0:T(512)S(1)}, u32[]{:S(2)}) copy-start(f32[432]{0:T(512)S(1)} %get-tuple-element.23) | copy-start | bytes 5188
  361.8 82.2 %copy-start.5 = (f32[432]{0:T(512)}, f32[432]{0:T(512)S(1)}, u32[]{:S(2)}) copy-start(f32[432]{0:T(512)S(1)} %get-tuple-element.24) | copy-start | bytes 5188
  361.8 80.9 %copy-start.2 = (f32[640]{0:T(1024)}, f32[640]{0:T(1024)S(1)}, u32[]{:S(2)}) copy-start(f32[640]{0:T(1024)S(1)} %get-tuple-element.21) | copy-start | bytes 7684
  361.8 82.1 %copy-start.3 = (f32[640]{0:T(1024)}, f32[640]{0:T(1024)S(1)}, u32[]{:S(2)}) copy-start(f32[640]{0:T(1024)S(1)} %get-tuple-element.22) | copy-start | bytes 7684
Sparse Core Ops, SparseCore 0:
  10.6 56.6 all-gather.4
  74.8 48.1 reduce-scatter.2
  125.7 47.8 all-gather.6
  176.0 47.2 all-gather.10
  226.0 51.4 all-gather.8
  282.5 89.6 reduce-scatter.4
where the time goes:
time: 452 us
  waiting for transfers between devices  246 us (54%)
  blocking collectives  155 us (34%)
  matrix products  28.4 us (6%)
  between operations  15.6 us (3%)
  other arithmetic  7.26 us (2%)
    psum x1, blocking collectives, per_device(): lax.psum((jnp.sum(raw_in * raw_in), jnp.sum(raw_out * raw_out)), ('row',...  77.3 us
    psum x1, blocking collectives, per_device(): lax.psum((jnp.sum(square_in, axis=0), jnp.sum(square_out, axis=0)), 'row')  63.8 us
    all_gather x1, waiting for transfers between devices, per_device(): lax.all_gather(grad_out, 'row', axis=0, tiled=True)  59.3 us
    reduce_scatter x1, waiting for transfers between devices, per_device(): lax.psum_scatter(contract_last(rows_here, w_out).astype(jnp.bfloat16), 'c...  48.2 us
    all_gather x1, waiting for transfers between devices, per_device(): lax.all_gather(inputs, 'row', axis=0, tiled=True)  47.6 us
    all_gather x1, waiting for transfers between devices, per_device(): lax.all_gather(pre_grad, 'col', axis=0, tiled=True)  46.8 us
    all_gather x1, waiting for transfers between devices, per_device(): lax.all_gather(act, 'col', axis=0, tiled=True)  41.8 us
    psum x1, blocking collectives, per_device(): lax.psum((jnp.sum(square_in, axis=1), jnp.sum(square_out, axis=1)), 'col')  13.8 us
  transfers between devices with their start and end apart: 6, of which 5 were waited for; matrix products, arithmetic and copies ran while one was open for 6% of the time, Pallas kernels for 0%

commit v1 on v0

--- a/solution.py
+++ b/solution.py
@@ -80,7 +80,7 @@
     col_out = col_moment(col_sums[1], col_out_prev)
     raw_in = grad_w_in / jnp.sqrt(row_in[:, None] * col_in[None, :] / token_count)
     raw_out = grad_w_out / jnp.sqrt(row_out[:, None] * col_out[None, :] / token_count)
-    norms = lax.psum((jnp.sum(raw_in * raw_in), jnp.sum(raw_out * raw_out)), ("row", "col"))
+    norms = lax.psum(lax.psum((jnp.sum(raw_in * raw_in), jnp.sum(raw_out * raw_out)), "col"), "row")
     total_in = norms[0]
     total_out = norms[1]
     rms_in = jnp.sqrt(total_in / (FF * D))

time: 452 us -> 460 us (1.018)
  blocking collectives: 155 us -> 163 us
    psum x1 -> x2, blocking collectives: 77.3 us -> 85.1 us  [the longest x1 73 us: per_device(): lax.psum(lax.psum((jnp.sum(raw_in * raw_in), jnp.sum(raw_out * raw_out)),...]
where the time goes in v1:
time: 460 us
  waiting for transfers between devices  246 us (53%)
  blocking collectives  163 us (35%)
  matrix products  28.4 us (6%)
  between operations  15.6 us (3%)
  other arithmetic  7.26 us (2%)
    psum x1, blocking collectives, per_device(): lax.psum(lax.psum((jnp.sum(raw_in * raw_in), jnp.sum(raw_out * raw_out)),...  73 us
    psum x1, blocking collectives, per_device(): lax.psum((jnp.sum(square_in, axis=0), jnp.sum(square_out, axis=0)), 'row')  63.8 us
    all_gather x1, waiting for transfers between devices, per_device(): lax.all_gather(grad_out, 'row', axis=0, tiled=True)  59.3 us
    reduce_scatter x1, waiting for transfers between devices, per_device(): lax.psum_scatter(contract_last(rows_here, w_out).astype(jnp.bfloat16), 'c...  48.2 us
    all_gather x1, waiting for transfers between devices, per_device(): lax.all_gather(inputs, 'row', axis=0, tiled=True)  47.6 us
    all_gather x1, waiting for transfers between devices, per_device(): lax.all_gather(pre_grad, 'col', axis=0, tiled=True)  46.8 us
    all_gather x1, waiting for transfers between devices, per_device(): lax.all_gather(act, 'col', axis=0, tiled=True)  41.8 us
    psum x1, blocking collectives, per_device(): lax.psum((jnp.sum(square_in, axis=1), jnp.sum(square_out, axis=1)), 'col')  13.8 us
  transfers between devices with their start and end apart: 6, of which 5 were waited for; matrix products, arithmetic and copies ran while one was open for 6% of the time, Pallas kernels for 0%

profile of v1, /device:TPU:1, one launch (start us, length us, event | category | flops | bytes accessed | tf_op | source)
XLA Modules:
  0.0 459.8 jit_solution(15840917870155832336)
XLA Ops:
  7.2 0.0 copy-start
  7.2 0.0 all-gather.5.cloned.1.call-start
  7.2 0.7 all-gather.5.cloned.1.call-update
  7.9 0.0 reduce-scatter.3.cloned.1.call-start
  8.0 59.3 %all-gather.5.cloned.1.call-done = bf16[4096,640]{1,0:T(8,128)(2,1)} async-done(((bf16[128,640]{1,0:T(8,128)(2,1)}), bf16[4096,640]{1,0:T(8,128)(2,1)}) %all-gather.5.cloned.1.call-update) | async-done | bytes 5242896 | tf_op jit(solution)/shard_map/all_gather | solution.py:49
  67.3 7.4 %convolution_convert_fusion.1 = bf16[4096,432]{0,1:T(8,128)(2,1)} fusion(bf16[4096,640]{1,0:T(8,128)(2,1)} %all-gather.5.cloned.1.call-done, bf16[432,640]{1,0:T(8,128)(2,1)} %param.13), kind=kOutput, calls=%fused_computation.1 | convolution fusion | flops 2266693632 | bytes 9334784 | tf_op jit(solution)/shard_map/dot_general | solution.py:26
  74.7 0.0 reduce-scatter.3.cloned.1.call-update
  74.7 0.0 all-gather.7.cloned.1.call-start
  74.7 48.2 %reduce-scatter.3.cloned.1.call-done = bf16[512,432]{0,1:T(8,128)(2,1)} async-done(((bf16[4096,432]{0,1:T(8,128)(2,1)}), bf16[512,432]{0,1:T(8,128)(2,1)}) %reduce-scatter.3.cloned.1.call-update) | async-done | bytes 442384 | tf_op jit(solution)/shard_map/reduce_scatter | solution.py:54
  123.0 2.6 fusion.7
  125.6 0.0 all-gather.7.cloned.1.call-update
  125.6 0.0 all-gather.11.cloned.1.call-start
  125.6 0.5 all-gather.11.cloned.1.call-update
  126.2 0.0 all-gather.9.cloned.1.call-start
  126.2 0.5 all-gather.9.cloned.1.call-update
  126.8 0.0 reduce-scatter.5.cloned.1.call-start
  126.8 46.8 %all-gather.7.cloned.1.call-done = bf16[4096,432]{0,1:T(8,128)(2,1)} async-done(((bf16[512,432]{0,1:T(8,128)(2,1)}), bf16[4096,432]{0,1:T(8,128)(2,1)}) %all-gather.7.cloned.1.call-update) | async-done | bytes 3538960 | tf_op jit(solution)/shard_map/all_gather | solution.py:62
  173.6 7.9 %convolution_convert_fusion = bf16[4096,640]{1,0:T(8,128)(2,1)} fusion(bf16[4096,432]{0,1:T(8,128)(2,1)} %all-gather.7.cloned.1.call-done, bf16[432,640]{1,0:T(8,128)(2,1)S(1)} %copy-done), kind=kOutput, calls=%fused_computation | convolution fusion | flops 2267545600 | bytes 9334784 | tf_op jit(solution)/shard_map/dot_general | solution.py:68
  181.5 0.0 reduce-scatter.5.cloned.1.call-update
  181.5 41.8 %all-gather.11.cloned.1.call-done = bf16[4096,432]{0,1:T(8,128)(2,1)} async-done(((bf16[512,432]{0,1:T(8,128)(2,1)}), bf16[4096,432]{0,1:T(8,128)(2,1)}) %all-gather.11.cloned.1.call-update) | async-done | bytes 3538960 | tf_op jit(solution)/shard_map/all_gather | solution.py:61
  223.3 6.6 %multiply_reduce_fusion.3 = (f32[432]{0:T(512)S(1)}, f32[640]{0:T(1024)S(1)}, f32[432,640]{1,0:T(8,128)S(1)}) fusion(bf16[4096,432]{0,1:T(8,128)(2,1)} %all-gather.11.cloned.1.call-done, bf16[4096,640]{1,0:T(8,128)(2,1)} %all-gather.5.cloned.1.call-done), kind=kOutput, calls=%fused_computation.16 | convolution fusion | flops 2265752576 | bytes 9892032 | tf_op jit(solution)/shard_map/dot_general | solution.py:32
  229.9 47.6 %all-gather.9.cloned.1.call-done = bf16[4096,640]{1,0:T(8,128)(2,1)} async-done(((bf16[128,640]{1,0:T(8,128)(2,1)}), bf16[4096,640]{1,0:T(8,128)(2,1)}) %all-gather.9.cloned.1.call-update) | async-done | bytes 5242896 | tf_op jit(solution)/shard_map/all_gather | solution.py:50
  277.5 6.6 %multiply_reduce_fusion.5 = (f32[432]{0:T(512)S(1)}, f32[640]{0:T(1024)S(1)}, f32[432,640]{1,0:T(8,128)S(1)}) fusion(bf16[4096,432]{0,1:T(8,128)(2,1)} %all-gather.7.cloned.1.call-done, bf16[4096,640]{1,0:T(8,128)(2,1)} %all-gather.9.cloned.1.call-done), kind=kOutput, calls=%fused_computation.18 | convolution fusion | flops 2265752576 | bytes 9892032 | tf_op jit(solution)/shard_map/dot_general | solution.py:32
  284.1 63.8 %all-reduce.1 = (f32[640]{0:T(1024)S(1)}, f32[640]{0:T(1024)S(1)}) all-reduce(f32[640]{0:T(1024)S(1)} %get-tuple-element.10, f32[640]{0:T(1024)S(1)} %get-tuple-element.8), channel_id=1, replica_groups=mesh['row'=32,'col'=8] {'row'}, use_global_device_ids=true, to_apply=%region_5.0 | all-reduce | flops 1280 | bytes 10240 | tf_op jit(solution)/shard_map/psum | solution.py:78
  347.9 13.8 %all-reduce.3 = (f32[432]{0:T(512)S(1)}, f32[432]{0:T(512)S(1)}) all-reduce(f32[432]{0:T(512)S(1)} %get-tuple-element.9, f32[432]{0:T(512)S(1)} %get-tuple-element.7), channel_id=1, replica_groups=mesh['row'=32,'col'=8] {'col'}, use_global_device_ids=true, to_apply=%region_3.0 | all-reduce | flops 864 | bytes 6912 | tf_op jit(solution)/shard_map/psum | solution.py:75
  361.8 0.0 copy-start.5
  361.8 1.1 multiply_reduce_fusion
  362.9 1.1 multiply_reduce_fusion.1
  364.0 12.1 %all-reduce.2 = (f32[]{:T(128)}, f32[]{:T(128)}) all-reduce(f32[]{:T(128)} %multiply_reduce_fusion.1, f32[]{:T(128)} %multiply_reduce_fusion), channel_id=1, replica_groups=mesh['row'=32,'col'=8] {'col'}, use_global_device_ids=true, to_apply=%region_7.0 | all-reduce | flops 2 | bytes 16 | tf_op jit(solution)/shard_map/psum | solution.py:83
  376.1 73.0 %all-reduce = (f32[]{:T(128)}, f32[]{:T(128)}) all-reduce(f32[]{:T(128)} %get-tuple-element.15, f32[]{:T(128)} %get-tuple-element.16), channel_id=1, replica_groups=mesh['row'=32,'col'=8] {'row'}, use_global_device_ids=true, to_apply=%region_8.0 | all-reduce | flops 2 | bytes 16 | tf_op jit(solution)/shard_map/psum | solution.py:83
  450.5 1.2 fusion.12
  451.8 1.2 fusion.11
  (21 shorter events, 0.1 us)
Async XLA Ops:
  7.2 166.5 %copy-start = (bf16[432,640]{1,0:T(8,128)(2,1)S(1)}, bf16[432,640]{1,0:T(8,128)(2,1)}, u32[]{:S(2)}) copy-start(bf16[432,640]{1,0:T(8,128)(2,1)} %param.12) | copy-start | bytes 1658884
  7.2 60.1 %all-gather.5.cloned.1.call-start = ((), (), s32[]{:S(2)}) async-start(), calls=%async_computation.2 | async-start | bytes 5406720 | tf_op jit(solution)/shard_map/all_gather | solution.py:49
  7.9 115.1 %reduce-scatter.3.cloned.1.call-start = ((), (), s32[]{:S(2)}) async-start(), calls=%async_computation.3 | async-start | bytes 3981312 | tf_op jit(solution)/shard_map/reduce_scatter | solution.py:54
  74.7 48.3 %copy-start.1 = (bf16[512,432]{0,1:T(8,128)(2,1)S(1)}, bf16[512,432]{0,1:T(8,128)(2,1)}, u32[]{:S(2)}) copy-start(bf16[512,432]{0,1:T(8,128)(2,1)} %param.11) | copy-start | bytes 1327108
  74.7 98.9 %all-gather.7.cloned.1.call-start = ((), (), s32[]{:S(2)}) async-start(), calls=%async_computation.4 | async-start | bytes 3981312 | tf_op jit(solution)/shard_map/all_gather | solution.py:62
  125.6 97.7 %all-gather.11.cloned.1.call-start = ((), (), s32[]{:S(2)}) async-start(), calls=%async_computation.7 | async-start | bytes 3981312 | tf_op jit(solution)/shard_map/all_gather | solution.py:61
  126.2 151.4 %all-gather.9.cloned.1.call-start = ((), (), s32[]{:S(2)}) async-start(), calls=%async_computation.6 | async-start | bytes 5406720 | tf_op jit(solution)/shard_map/all_gather | solution.py:50
  126.8 326.2 %reduce-scatter.5.cloned.1.call-start = ((), (), s32[]{:S(2)}) async-start(), calls=%async_computation.5 | async-start | bytes 5406720 | tf_op jit(solution)/shard_map/reduce_scatter | solution.py:67
  229.9 131.9 %copy-start.8 = (f32[432]{0:T(512)S(1)}, f32[432]{0:T(512)}, u32[]{:S(2)}) copy-start(f32[432]{0:T(512)} %param.16) | copy-start | bytes 5188
  229.9 131.9 %copy-start.9 = (f32[432]{0:T(512)S(1)}, f32[432]{0:T(512)}, u32[]{:S(2)}) copy-start(f32[432]{0:T(512)} %param.14) | copy-start | bytes 5188
  229.9 131.9 %copy-start.6 = (f32[640]{0:T(1024)S(1)}, f32[640]{0:T(1024)}, u32[]{:S(2)}) copy-start(f32[640]{0:T(1024)} %param.17) | copy-start | bytes 7684
  229.9 131.9 %copy-start.7 = (f32[640]{0:T(1024)S(1)}, f32[640]{0:T(1024)}, u32[]{:S(2)}) copy-start(f32[640]{0:T(1024)} %param.15) | copy-start | bytes 7684
  361.8 88.7 %copy-start.4 = (f32[432]{0:T(512)}, f32[432]{0:T(512)S(1)}, u32[]{:S(2)}) copy-start(f32[432]{0:T(512)S(1)} %get-tuple-element.25) | copy-start | bytes 5188
  361.8 90.0 %copy-start.5 = (f32[432]{0:T(512)}, f32[432]{0:T(512)S(1)}, u32[]{:S(2)}) copy-start(f32[432]{0:T(512)S(1)} %get-tuple-element.26) | copy-start | bytes 5188
  361.8 88.7 %copy-start.2 = (f32[640]{0:T(1024)}, f32[640]{0:T(1024)S(1)}, u32[]{:S(2)}) copy-start(f32[640]{0:T(1024)S(1)} %get-tuple-element.23) | copy-start | bytes 7684
  361.8 89.9 %copy-start.3 = (f32[640]{0:T(1024)}, f32[640]{0:T(1024)S(1)}, u32[]{:S(2)}) copy-start(f32[640]{0:T(1024)S(1)} %get-tuple-element.24) | copy-start | bytes 7684
Sparse Core Ops, SparseCore 0:
  10.6 56.6 all-gather.4
  74.8 48.1 reduce-scatter.2
  125.7 47.8 all-gather.6
  176.0 47.2 all-gather.10
  226.0 51.4 all-gather.8
  282.5 89.6 reduce-scatter.4
